TPU v7x, 128 devices: a whole 4x4x4 slice. The times are simulated.
128 devices in a mesh: adapter: 32 (over y, x, core), mp: 4 (over z).
Axes of the slice: x: 4, y: 4, z: 4, core: 2. Of those that a mesh axis runs over, the one named last changes fastest.
Arguments:
- hidden: bfloat16 [8192, 4096], P('adapter', 'mp'), may hold values from -8 to 8
- subsets: int32 [8192, 8], P('adapter'), may hold values from 0 to 31, all different within a row; in each aligned block of 256 rows (0 to 255, 256 to 511, ...) at most 128 rows name the same one
- down_weight: bfloat16 [32, 4096, 256], P('adapter', 'mp'), may hold values from -0.09375 to 0.09375
- up_weight: bfloat16 [32, 256, 4096], P('adapter', None, 'mp'), may hold values from -0.375 to 0.375
- query_weight: bfloat16 [4096, 4096], P('mp'), may hold values from -0.08 to 2.08
- key_weight: bfloat16 [4096, 4096], P('mp'), may hold values from -0.08 to 2.08
Outputs:
- joined: bfloat16 [8192, 4096], P('adapter', 'mp')
Inputs may be any that keep to these rules, and one draw needn't show every extreme that they name: `subsets`: each row names 8 different adapters; within the rows of one index of the adapter axis no adapter is named by more than 128 rows.
All inputs are finite; a program needn't handle non-finite values.
Results may differ from a plain program's by a relative error of at most 0.025.
Values may be sent and summed in bfloat16 or wider, within the bound.
No kernel may reach another device: no remote copies, remote signals or barrier semaphores. Data moves between devices by JAX's collectives and lax.ppermute only.
A program may use at most 192 MiB of HBM per device.

v0:
```python
import jax
import jax.numpy as jnp
from jax import lax
from jax.sharding import PartitionSpec as P

D = 4096


def sent_to_all(x, axis):
    size = lax.axis_size(axis)
    return lax.all_to_all(jnp.broadcast_to(x[None], (size, *x.shape)), axis, 0, 0, tiled=True)


def over_copies(x, axis):
    return sent_to_all(x, axis).astype(jnp.float32).sum(axis=0)


def split_up(x, dim, size):
    before, after = (x.shape[:dim], x.shape[dim + 1 :])
    return jnp.moveaxis(x.reshape(*before, size, -1, *after), dim, 0)


def sent_and_summed(x, axis, dim):
    size = lax.axis_size(axis)
    parts = lax.all_to_all(split_up(x, dim, size), axis, 0, 0, tiled=True)
    return jnp.sum(parts.astype(jnp.float32), axis=0)


def in_order(parts, dim):
    parts = jnp.moveaxis(parts, 0, dim)
    shape = parts.shape
    return parts.reshape(*shape[:dim], shape[dim] * shape[dim + 1], *shape[dim + 2 :])


def collect(x, axis, dim):
    parts = sent_to_all(x, axis)
    return in_order(parts, dim)


def taken_together(x, axis):
    return sent_to_all(x, axis).sum(axis=0)


def tally(partial_sum):
    summed = over_copies(partial_sum.astype(jnp.bfloat16), "mp").astype(jnp.float32)
    return jnp.maximum(summed, 0.0).astype(jnp.bfloat16)


def per_device(hidden, subsets, down_weight, up_weight, query_weight, key_weight):
    row_count, width_local = hidden.shape
    fanout = subsets.shape[1]
    total_adapters = lax.axis_size("adapter") * down_weight.shape[0]
    capacity = min(row_count, 2 * row_count * fanout // total_adapters)
    labels = jnp.arange(total_adapters, dtype=jnp.int32)
    picks = (subsets[:, :, None] == labels[None, None, :]).astype(jnp.int32)
    chosen = jnp.sum(picks, axis=1)
    before = jnp.cumsum(chosen, axis=0) - chosen
    slot_rank = jnp.sum(picks * before[:, None, :], axis=2)
    flat_slot = subsets * capacity + slot_rank
    row_ids = jnp.broadcast_to(jnp.arange(row_count, dtype=jnp.int32)[:, None], flat_slot.shape)
    source_row = (
        jnp.zeros((total_adapters * capacity,), jnp.int32)
        .at[flat_slot.reshape(-1)]
        .set(row_ids.reshape(-1))
    )
    filled = jnp.zeros((total_adapters * capacity,), jnp.bool_).at[flat_slot.reshape(-1)].set(True)
    outgoing = jnp.where(
        filled[:, None], jnp.take(hidden, source_row, axis=0), jnp.zeros((), jnp.bfloat16)
    )
    outgoing = outgoing.reshape(total_adapters, capacity, width_local)
    query_part = jnp.dot(hidden, query_weight, preferred_element_type=jnp.float32)
    query_piece = sent_and_summed(query_part.astype(jnp.bfloat16), "mp", 1).astype(jnp.bfloat16)
    query = collect(query_piece, "mp", 1)
    probe = lax.dot_general(
        query, key_weight, (((1,), (1,)), ((), ())), preferred_element_type=jnp.float32
    ).astype(jnp.bfloat16)
    block = outgoing
    bottle = tally(
        jnp.einsum(
            "ncd,ndb->ncb",
            block,
            lax.all_gather(down_weight, "adapter", axis=0, tiled=True),
            preferred_element_type=jnp.float32,
        )
    )
    block = bottle
    returned = jnp.einsum(
        "ncb,nbd->ncd",
        block,
        lax.all_gather(up_weight, "adapter", axis=0, tiled=True),
        preferred_element_type=jnp.float32,
    ).astype(jnp.bfloat16)
    picked = jnp.take(returned.reshape(total_adapters * capacity, width_local), flat_slot, axis=0)
    widened = picked.astype(jnp.float32)
    base = hidden.astype(jnp.float32)
    probe_wide = probe.astype(jnp.float32)
    own_term = jnp.sum(base * probe_wide, axis=1)
    partial_logit = (
        jnp.einsum("rkd,rd->rk", widened, probe_wide, precision=lax.Precision.HIGHEST)
        + own_term[:, None]
    )
    logits = taken_together(partial_logit, "mp") * D ** (-0.5)
    share = jax.nn.softmax(logits, axis=-1)
    joined = base + jnp.einsum("rk,rkd->rd", share, widened, precision=lax.Precision.HIGHEST)
    return joined.astype(jnp.bfloat16)


def solution(mesh):
    return jax.shard_map(
        per_device,
        mesh=mesh,
        in_specs=(
            P("adapter", "mp"),
            P("adapter", None),
            P("adapter", "mp", None),
            P("adapter", None, "mp"),
            P("mp", None),
            P("mp", None),
        ),
        out_specs=P("adapter", "mp"),
        check_vma=False,
    )
```

profile of v0, /device:TPU:0, one launch (start us, length us, event | category | flops | bytes accessed | tf_op | source)
XLA Modules:
  0.0 257.7 jit_solution(9191249026218513655)
XLA Ops:
  6.5 0.7 all-gather.3.cloned.1.call-update
  7.3 0.7 all-gather.5.cloned.1.call-update
  8.0 5.9 %convolution_convert_fusion.1 = bf16[256,4096]{1,0:T(8,128)(2,1)S(1)} fusion(bf16[256,1024]{1,0:T(8,128)(2,1)} %param.6, bf16[1024,4096]{1,0:T(8,128)(2,1)} %param.10), kind=kOutput, calls=%fused_computation.11 | convolution fusion | flops 2148532224 | bytes 11010048 | tf_op jit(solution)/shard_map/dot_general | solution.py:71
  13.9 1.6 copy.58
  15.5 5.4 %all-to-all-start.1 = ((bf16[4,256,1024]{2,1,0:T(8,128)(2,1)}), bf16[4,256,1024]{2,1,0:T(8,128)(2,1)S(1)}, u32[]{:S(2)}, u32[]{:S(2)}) async-start(bf16[4,256,1024]{2,1,0:T(8,128)(2,1)} %bitcast.53), calls=%async_computation.1 | async-start | bytes 4194304 | tf_op jit(solution)/shard_map/all_to_all | solution.py:25
  21.0 0.6 reduce-window.6
  21.5 0.2 slice_reduce_fusion
  21.9 0.1 copy.39
  22.1 0.1 reshape.87
  22.3 8.1 %scatter_custom_fusion.1 = s32[4096]{0:T(1024)S(1)} fusion(s32[2048]{0:T(1024)S(1)} %bitcast.55, s32[2048]{0:T(1024)S(1)} %reshape.120, s32[]{:T(128)} %constant.18.clone.1), kind=kCustom, calls=%fused_computation.45 | custom fusion | bytes 16388 | tf_op jit(solution)/shard_map/scatter | solution.py:64
  30.4 18.2 %gather_fusion = bf16[4096,1024]{1,0:T(8,128)(2,1)} fusion(bf16[256,1024]{1,0:T(8,128)(2,1)S(1)} %copy-done, s32[4096]{0:T(1024)S(1)} %fusion.19), kind=kCustom, calls=%fused_computation | custom fusion | bytes 16793600 | tf_op jit(solution)/shard_map/jit(_take)/gather | solution.py:68
  48.7 9.1 %scatter_custom_fusion = pred[4096]{0:T(1024)(128)(4,1)S(1)} fusion(s32[2048]{0:T(1024)S(1)} %bitcast.56, pred[2048]{0:T(1024)(128)(4,1)S(1)} %broadcast.50, pred[]{:T(512)} %constant.27.clone.1), kind=kCustom, calls=%fused_computation.48 | custom fusion | bytes 4097 | tf_op jit(solution)/shard_map/scatter | solution.py:66
  57.8 0.4 reduce_sum.69
  58.2 0.2 copy.43
  58.4 1.4 broadcast_in_dim.97
  59.9 4.8 %all-to-all-start.2 = ((bf16[4,256,1024]{1,2,0:T(8,128)(2,1)}), bf16[4,256,1024]{1,2,0:T(8,128)(2,1)}, u32[]{:S(2)}, u32[]{:S(2)}) async-start(bf16[4,256,1024]{1,2,0:T(8,128)(2,1)} %broadcast_in_dim.97), calls=%async_computation.2 | async-start | bytes 4194304 | tf_op jit(solution)/shard_map/all_to_all | solution.py:11
  64.7 19.8 %all-gather.3.cloned.1.call-done = bf16[32,1024,256]{2,1,0:T(8,128)(2,1)} async-done(((bf16[1,1024,256]{2,1,0:T(8,128)(2,1)}), bf16[32,1024,256]{2,1,0:T(8,128)(2,1)}) %all-gather.3.cloned.1.call-update) | async-done | bytes 16777232 | tf_op jit(solution)/shard_map/all_gather | solution.py:82
  84.5 9.7 %fusion.12 = bf16[32,128,256]{2,1,0:T(8,128)(2,1)S(1)} fusion(bf16[32,1024,256]{2,1,0:T(8,128)(2,1)} %all-gather.3.cloned.1.call-done, bf16[32,128,1024]{2,1,0:T(8,128)(2,1)} %bitcast.52, pred[32,128]{1,0:T(8,128)(4,1)S(1)} %and_bitcast_fusion, pred[32,128]{1,0:T(8,128)(4,1)S(1)} %bitcast.57), kind=kOutput, calls=%fused_computation.22 | convolution fusion | flops 2156920832 | bytes 27271168 | tf_op jit(solution)/shard_map/ncd,ndb->ncb/dot_general | solution.py:79
  94.2 4.3 %broadcast_in_dim.94 = bf16[4,32,128,256]{3,2,1,0:T(8,128)(2,1)} broadcast(bf16[32,128,256]{2,1,0:T(8,128)(2,1)S(1)} %fusion.12), dimensions={1,2,3} | broadcast | bytes 10485760 | tf_op jit(solution)/shard_map/broadcast_in_dim | solution.py:11
  98.4 5.8 %all-to-all-start = ((bf16[4,32,128,256]{3,2,1,0:T(8,128)(2,1)}), bf16[4,32,128,256]{3,2,1,0:T(8,128)(2,1)}, u32[]{:S(2)}, u32[]{:S(2)}) async-start(bf16[4,32,128,256]{3,2,1,0:T(8,128)(2,1)} %broadcast_in_dim.94), calls=%async_computation | async-start | bytes 16777216 | tf_op jit(solution)/shard_map/all_to_all | solution.py:11
  104.3 0.1 copy.40
  104.5 0.2 copy.38
  104.7 6.5 %fusion.15 = (f32[256]{0:T(256)S(1)}, bf16[256,1024]{1,0:T(8,128)(2,1)S(1)}) fusion(bf16[256,1024]{1,0:T(8,128)(2,1)S(1)} %copy-done, bf16[256,4096]{0,1:T(8,128)(2,1)} %bitcast.10, bf16[1024,4096]{1,0:T(8,128)(2,1)} %param.11), kind=kOutput, calls=%fused_computation.26 | convolution fusion | flops 2148794112 | bytes 11535360 | tf_op jit(solution)/shard_map/dot_general | solution.py:74
  111.3 87.5 %all-to-all-done = bf16[4,32,128,256]{3,2,1,0:T(8,128)(2,1)} async-done(((bf16[4,32,128,256]{3,2,1,0:T(8,128)(2,1)}), bf16[4,32,128,256]{3,2,1,0:T(8,128)(2,1)}, u32[]{:S(2)}, u32[]{:S(2)}) %all-to-all-start) | async-done | bytes 8388640 | tf_op jit(solution)/shard_map/all_to_all | solution.py:11
  198.8 4.9 %convert_reduce_fusion = bf16[32,128,256]{2,1,0:T(8,128)(2,1)S(1)} fusion(bf16[4,32,128,256]{3,2,1,0:T(8,128)(2,1)} %all-to-all-done), kind=kLoop, calls=%fused_computation.4 | loop fusion | flops 7340032 | bytes 10485760 | tf_op jit(solution)/shard_map/reduce_sum | solution.py:15
  203.8 11.4 %convolution_convert_fusion = bf16[32,128,1024]{2,1,0:T(8,128)(2,1)} fusion(bf16[32,256,1024]{2,1,0:T(8,128)(2,1)} %all-gather.5.cloned.1.call-done, bf16[32,128,256]{2,1,0:T(8,128)(2,1)S(1)} %convert_reduce_fusion), kind=kOutput, calls=%fused_computation.10 | convolution fusion | flops 2154823680 | bytes 27262976 | tf_op jit(solution)/shard_map/ncb,nbd->ncd/dot_general | solution.py:87
  215.1 15.4 %gather_fusion.1 = bf16[2048,1024]{1,0:T(8,128)(2,1)} fusion(bf16[4096,1024]{1,0:T(8,128)(2,1)} %bitcast.51, s32[2048]{0:T(1024)S(1)} %broadcast_clamp_fusion), kind=kCustom, calls=%fused_computation.1 | custom fusion | bytes 8396800 | tf_op jit(solution)/shard_map/jit(_take)/gather | solution.py:93
  230.6 5.3 %fusion.8 = f32[256,1,8]{2,1,0:T(1,128)S(1)} fusion(bf16[2048,1024]{1,0:T(8,128)(2,1)} %gather_fusion.1, pred[256,8]{1,0:T(8,128)(4,1)S(1)} %copy.38, bf16[256,1024,1]{1,0,2:T(8,128)(2,1)S(1)} %bitcast.58), kind=kOutput, calls=%fused_computation.17 | convolution fusion | flops 6291456 | bytes 4728832 | tf_op jit(solution)/shard_map/rkd,rd->rk/dot_general | solution.py:99
  236.0 7.8 %all_to_all.20 = f32[4,256,8]{1,2,0:T(8,128)S(1)} all-to-all(f32[4,256,8]{1,2,0:T(8,128)S(1)} %broadcast_in_dim.98), channel_id=1, replica_groups=mesh['adapter'=32,'mp'=4] {'mp'}, dimensions={0} | all-to-all | bytes 65536 | tf_op jit(solution)/shard_map/all_to_all | solution.py:11
  243.8 0.1 copy.46
  244.0 5.8 %fusion.7 = f32[256,1,1024]{2,1,0:T(1,128)S(1)} fusion(f32[256,8,1]{1,2,0:T(1,128)S(1)} %copy.46, bf16[2048,1024]{1,0:T(8,128)(2,1)} %gather_fusion.1, pred[256,8]{1,0:T(8,128)(4,1)S(1)} %copy.38), kind=kOutput, calls=%fused_computation.16 | convolution fusion | flops 27262976 | bytes 5253120 | tf_op jit(solution)/shard_map/rk,rkd->rd/dot_general | solution.py:104
  249.8 1.1 fusion.16
  (32 shorter events, 0.7 us)
Async XLA Ops:
  6.5 77.9 %all-gather.3.cloned.1.call-start = ((), (), s32[]{:S(2)}) async-start(), calls=%async_computation.4 | async-start | bytes 17301504 | tf_op jit(solution)/shard_map/all_gather | solution.py:82
  7.3 196.5 %all-gather.5.cloned.1.call-start = ((), (), s32[]{:S(2)}) async-start(), calls=%async_computation.5 | async-start | bytes 17301504 | tf_op jit(solution)/shard_map/all_gather | solution.py:90
  13.9 7.0 %copy-start.1 = (s32[256,8]{0,1:T(8,128)S(1)}, s32[256,8]{0,1:T(8,128)}, u32[]{:S(2)}) copy-start(s32[256,8]{0,1:T(8,128)} %param.7) | copy-start | bytes 24580
  13.9 16.5 %copy-start = (bf16[256,1024]{1,0:T(8,128)(2,1)S(1)}, bf16[256,1024]{1,0:T(8,128)(2,1)}, u32[]{:S(2)}) copy-start(bf16[256,1024]{1,0:T(8,128)(2,1)} %param.6) | copy-start | bytes 1572868
  15.5 42.3 %all-to-all-start.1 = ((bf16[4,256,1024]{2,1,0:T(8,128)(2,1)}), bf16[4,256,1024]{2,1,0:T(8,128)(2,1)S(1)}, u32[]{:S(2)}, u32[]{:S(2)}) async-start(bf16[4,256,1024]{2,1,0:T(8,128)(2,1)} %bitcast.53), calls=%async_computation.1 | async-start | bytes 4194304 | tf_op jit(solution)/shard_map/all_to_all | solution.py:25
  59.9 34.3 %all-to-all-start.2 = ((bf16[4,256,1024]{1,2,0:T(8,128)(2,1)}), bf16[4,256,1024]{1,2,0:T(8,128)(2,1)}, u32[]{:S(2)}, u32[]{:S(2)}) async-start(bf16[4,256,1024]{1,2,0:T(8,128)(2,1)} %broadcast_in_dim.97), calls=%async_computation.2 | async-start | bytes 4194304 | tf_op jit(solution)/shard_map/all_to_all | solution.py:11
  98.4 100.4 %all-to-all-start = ((bf16[4,32,128,256]{3,2,1,0:T(8,128)(2,1)}), bf16[4,32,128,256]{3,2,1,0:T(8,128)(2,1)}, u32[]{:S(2)}, u32[]{:S(2)}) async-start(bf16[4,32,128,256]{3,2,1,0:T(8,128)(2,1)} %broadcast_in_dim.94), calls=%async_computation | async-start | bytes 16777216 | tf_op jit(solution)/shard_map/all_to_all | solution.py:11
Sparse Core Ops, SparseCore 0:
  9.6 74.8 all-gather.2
  86.7 71.8 all-gather.4
where the time goes:
time: 258 us
  waiting for transfers between devices  109 us (42%)
  local copies, waits for them, and re-layouts  59.5 us (23%)
  matrix products  44.6 us (17%)
  starting transfers between devices  16.1 us (6%)
  between operations  13.6 us (5%)
  blocking collectives  7.81 us (3%)
  other arithmetic  7.31 us (3%)
    all_to_all x2, waiting for transfers between devices, sent_to_all(): lax.all_to_all(jnp.broadcast_to(x[None], (size, *x.shape)), axis, 0, 0, t...  87.5 us
    all_gather x1, waiting for transfers between devices, per_device(): lax.all_gather(down_weight, 'adapter', axis=0, tiled=True)  19.8 us
    gather x1, local copies, waits for them, and re-layouts, per_device(): jnp.take(hidden, source_row, axis=0)  18.2 us
    gather x1, local copies, waits for them, and re-layouts, per_device(): jnp.take(returned.reshape(total_adapters * capacity, width_local), flat_s...  15.4 us
    dot_general x1, matrix products, per_device(): jnp.einsum('ncb,nbd->ncd', block, lax.all_gather(up_weight, 'adapter', ax...  11.4 us
    all_to_all x2, starting transfers between devices, sent_to_all(): lax.all_to_all(jnp.broadcast_to(x[None], (size, *x.shape)), axis, 0, 0, t...  10.6 us
    dot_general x1, matrix products, per_device(): jnp.einsum('ncd,ndb->ncb', block, lax.all_gather(down_weight, 'adapter',...  9.7 us
    scatter x1, local copies, waits for them, and re-layouts, per_device(): jnp.zeros((total_adapters * capacity,), jnp.bool_).at[flat_slot.reshape(-1)]  9.12 us
  transfers between devices with their start and end apart: 5, of which 2 were waited for; matrix products, arithmetic and copies ran while one was open for 28% of the time, Pallas kernels for 0%

commit v1 on v0

--- a/solution.py
+++ b/solution.py
@@ -1,9 +1,22 @@
+import functools
 import jax
 import jax.numpy as jnp
 from jax import lax
 from jax.sharding import PartitionSpec as P
 
 D = 4096
+
+
+def pair_the_joints(body, on_dim):
+    return jnp.concatenate(
+        lax.all_to_all(
+            jnp.stack([body for _ in range(lax.axis_size("adapter"))], axis=0), "adapter", 0, 0
+        ),
+        axis=on_dim,
+    )
+
+
+_point_state = functools.partial(pair_the_joints, on_dim=0)
 
 
 def sent_to_all(x, axis):
@@ -77,10 +90,7 @@
     block = outgoing
     bottle = tally(
         jnp.einsum(
-            "ncd,ndb->ncb",
-            block,
-            lax.all_gather(down_weight, "adapter", axis=0, tiled=True),
-            preferred_element_type=jnp.float32,
+            "ncd,ndb->ncb", block, _point_state(down_weight), preferred_element_type=jnp.float32
         )
     )
     block = bottle

time: 258 us -> 479 us (1.86)
  the two profiles are of different devices: /device:TPU:0 before, /device:TPU:28 now
where the time goes in v1:
time: 479 us; the launch traced here: 478 us
  waiting for transfers between devices  291 us (61%)
  local copies, waits for them, and re-layouts  64.6 us (13%)
  matrix products  44.5 us (9%)
  blocking collectives  39.2 us (8%)
  starting transfers between devices  17.9 us (4%)
  between operations  13.7 us (3%)
  other arithmetic  7.31 us (2%)
    all_to_all x1, waiting for transfers between devices, pair_the_joints(): lax.all_to_all(jnp.stack([body for _ in range(lax.axis_size('adapter'))],...  187 us
    all_to_all x2, waiting for transfers between devices, sent_to_all(): lax.all_to_all(jnp.broadcast_to(x[None], (size, *x.shape)), axis, 0, 0, t...  103 us
    all_to_all x1, blocking collectives, sent_and_summed(): parts = lax.all_to_all(split_up(x, dim, size), axis, 0, 0, tiled=True)  31.4 us
    gather x1, local copies, waits for them, and re-layouts, per_device(): jnp.take(hidden, source_row, axis=0)  18.2 us
    gather x1, local copies, waits for them, and re-layouts, per_device(): jnp.take(returned.reshape(total_adapters * capacity, width_local), flat_s...  15.4 us
    dot_general x1, matrix products, per_device(): jnp.einsum('ncb,nbd->ncd', block, lax.all_gather(up_weight, 'adapter', ax...  11.4 us
    all_to_all x2, starting transfers between devices, sent_to_all(): lax.all_to_all(jnp.broadcast_to(x[None], (size, *x.shape)), axis, 0, 0, t...  10.3 us
    dot_general x1, matrix products, per_device(): jnp.einsum('ncd,ndb->ncb', block, _point_state(down_weight), preferred_el...  9.72 us
  transfers between devices with their start and end apart: 4, of which 3 were waited for; matrix products, arithmetic and copies ran while one was open for 16% of the time, Pallas kernels for 0%

profile of v1, /device:TPU:28, one launch (start us, length us, event | category | flops | bytes accessed | tf_op | source)
XLA Modules:
  0.0 478.0 jit_solution(7472549547056646404)
XLA Ops:
  6.5 0.7 all-gather.2.cloned.1.call-update
  7.3 5.9 %convolution_convert_fusion.1 = bf16[256,4096]{1,0:T(8,128)(2,1)S(1)} fusion(bf16[256,1024]{1,0:T(8,128)(2,1)} %param.6, bf16[1024,4096]{1,0:T(8,128)(2,1)} %param.10), kind=kOutput, calls=%fused_computation.12 | convolution fusion | flops 2148532224 | bytes 11010048 | tf_op jit(solution)/shard_map/dot_general | solution.py:84
  13.2 0.2 copy.58
  13.4 31.4 %all_to_all.25 = bf16[4,256,1024]{2,1,0:T(8,128)(2,1)S(1)} all-to-all(bf16[4,256,1024]{2,1,0:T(8,128)(2,1)S(1)} %bitcast.58), channel_id=1, replica_groups=mesh['adapter'=32,'mp'=4] {'mp'}, dimensions={0} | all-to-all | bytes 4194304 | tf_op jit(solution)/shard_map/all_to_all | solution.py:38
  44.8 6.5 %stack.2 = bf16[32,1,1024,256]{3,2,1,0:T(8,128)(2,1)} broadcast(bf16[1024,256]{1,0:T(8,128)(2,1)S(1)} %bitcast.60), dimensions={2,3} | broadcast | bytes 17301504 | tf_op jit(solution)/shard_map/stack | solution.py:13
  51.3 7.6 %all-to-all-start = ((bf16[32,1,1024,256]{3,2,1,0:T(8,128)(2,1)}), bf16[32,1,1024,256]{3,2,1,0:T(8,128)(2,1)}, u32[]{:S(2)}, u32[]{:S(2)}) async-start(bf16[32,1,1024,256]{3,2,1,0:T(8,128)(2,1)} %stack.2), calls=%async_computation | async-start | bytes 33554432 | tf_op jit(solution)/shard_map/all_to_all | solution.py:12
  58.9 0.6 reduce-window.6
  59.5 0.2 slice_reduce_fusion
  59.9 0.1 copy.39
  60.3 8.1 %scatter_custom_fusion.1 = s32[4096]{0:T(1024)S(1)} fusion(s32[2048]{0:T(1024)S(1)} %bitcast.61, s32[2048]{0:T(1024)S(1)} %reshape.127, s32[]{:T(128)} %constant.18.clone.1), kind=kCustom, calls=%fused_computation.46 | custom fusion | bytes 16388 | tf_op jit(solution)/shard_map/scatter | solution.py:77
  68.4 18.2 %gather_fusion = bf16[4096,1024]{1,0:T(8,128)(2,1)} fusion(bf16[256,1024]{1,0:T(8,128)(2,1)S(1)} %copy-done, s32[4096]{0:T(1024)S(1)} %fusion.22), kind=kCustom, calls=%fused_computation | custom fusion | bytes 16793600 | tf_op jit(solution)/shard_map/jit(_take)/gather | solution.py:81
  86.6 9.1 %scatter_custom_fusion = pred[4096]{0:T(1024)(128)(4,1)S(1)} fusion(s32[2048]{0:T(1024)S(1)} %bitcast.62, pred[2048]{0:T(1024)(128)(4,1)S(1)} %broadcast.53, pred[]{:T(512)} %constant.27.clone.1), kind=kCustom, calls=%fused_computation.49 | custom fusion | bytes 4097 | tf_op jit(solution)/shard_map/scatter | solution.py:79
  95.7 0.4 reduce_sum.69
  96.2 0.2 copy.43
  96.4 187.0 %all-to-all-done = bf16[32,1,1024,256]{3,2,1,0:T(8,128)(2,1)} async-done(((bf16[32,1,1024,256]{3,2,1,0:T(8,128)(2,1)}), bf16[32,1,1024,256]{3,2,1,0:T(8,128)(2,1)}, u32[]{:S(2)}, u32[]{:S(2)}) %all-to-all-start) | async-done | bytes 16777248 | tf_op jit(solution)/shard_map/all_to_all | solution.py:12
  283.4 1.5 broadcast_in_dim.97
  284.9 4.6 all-to-all-start.3
  289.5 9.7 %fusion.13 = bf16[32,128,256]{2,1,0:T(8,128)(2,1)S(1)} fusion(bf16[32,1,1024,256]{3,2,1,0:T(8,128)(2,1)} %all-to-all-done, bf16[32,128,1024]{2,1,0:T(8,128)(2,1)} %bitcast.57, pred[32,128]{1,0:T(8,128)(4,1)S(1)} %and_bitcast_fusion, pred[32,128]{1,0:T(8,128)(4,1)S(1)} %bitcast.63), kind=kOutput, calls=%fused_computation.23 | convolution fusion | flops 2156920832 | bytes 27271168 | tf_op jit(solution)/shard_map/ncd,ndb->ncb/dot_general | solution.py:92
  299.2 17.1 %all-to-all-done.3 = bf16[4,256,1024]{1,2,0:T(8,128)(2,1)} async-done(((bf16[4,256,1024]{1,2,0:T(8,128)(2,1)}), bf16[4,256,1024]{1,2,0:T(8,128)(2,1)}, u32[]{:S(2)}, u32[]{:S(2)}) %all-to-all-start.3) | async-done | bytes 2097184 | tf_op jit(solution)/shard_map/all_to_all | solution.py:24
  316.4 4.3 broadcast_in_dim.94
  320.6 5.7 %all-to-all-start.1 = ((bf16[4,32,128,256]{3,2,1,0:T(8,128)(2,1)}), bf16[4,32,128,256]{3,2,1,0:T(8,128)(2,1)}, u32[]{:S(2)}, u32[]{:S(2)}) async-start(bf16[4,32,128,256]{3,2,1,0:T(8,128)(2,1)} %broadcast_in_dim.94), calls=%async_computation.1 | async-start | bytes 16777216 | tf_op jit(solution)/shard_map/all_to_all | solution.py:24
  326.5 0.2 copy.38
  326.7 6.5 %fusion.18 = (f32[256]{0:T(256)S(1)}, bf16[256,1024]{1,0:T(8,128)(2,1)S(1)}) fusion(bf16[256,1024]{1,0:T(8,128)(2,1)S(1)} %copy-done, bf16[256,4096]{0,1:T(8,128)(2,1)} %bitcast.12, bf16[1024,4096]{1,0:T(8,128)(2,1)} %param.11), kind=kOutput, calls=%fused_computation.27 | convolution fusion | flops 2148794112 | bytes 11535360 | tf_op jit(solution)/shard_map/dot_general | solution.py:87
  333.2 86.0 %all-to-all-done.1 = bf16[4,32,128,256]{3,2,1,0:T(8,128)(2,1)} async-done(((bf16[4,32,128,256]{3,2,1,0:T(8,128)(2,1)}), bf16[4,32,128,256]{3,2,1,0:T(8,128)(2,1)}, u32[]{:S(2)}, u32[]{:S(2)}) %all-to-all-start.1) | async-done | bytes 8388640 | tf_op jit(solution)/shard_map/all_to_all | solution.py:24
  419.2 4.9 %convert_reduce_fusion = bf16[32,128,256]{2,1,0:T(8,128)(2,1)S(1)} fusion(bf16[4,32,128,256]{3,2,1,0:T(8,128)(2,1)} %all-to-all-done.1), kind=kLoop, calls=%fused_computation.6 | loop fusion | flops 7340032 | bytes 10485760 | tf_op jit(solution)/shard_map/reduce_sum | solution.py:28
  424.1 11.4 %convolution_convert_fusion = bf16[32,128,1024]{2,1,0:T(8,128)(2,1)} fusion(bf16[32,256,1024]{2,1,0:T(8,128)(2,1)} %all-gather.2.cloned.1.call-done, bf16[32,128,256]{2,1,0:T(8,128)(2,1)S(1)} %convert_reduce_fusion), kind=kOutput, calls=%fused_computation.11 | convolution fusion | flops 2154823680 | bytes 27262976 | tf_op jit(solution)/shard_map/ncb,nbd->ncd/dot_general | solution.py:97
  435.5 15.4 %gather_fusion.1 = bf16[2048,1024]{1,0:T(8,128)(2,1)} fusion(bf16[4096,1024]{1,0:T(8,128)(2,1)} %bitcast.56, s32[2048]{0:T(1024)S(1)} %broadcast_clamp_fusion), kind=kCustom, calls=%fused_computation.1 | custom fusion | bytes 8396800 | tf_op jit(solution)/shard_map/jit(_take)/gather | solution.py:103
  450.9 5.3 %fusion.9 = f32[256,1,8]{2,1,0:T(1,128)S(1)} fusion(bf16[2048,1024]{1,0:T(8,128)(2,1)} %gather_fusion.1, pred[256,8]{1,0:T(8,128)(4,1)S(1)} %copy.38, bf16[256,1024,1]{1,0,2:T(8,128)(2,1)S(1)} %bitcast.64), kind=kOutput, calls=%fused_computation.18 | convolution fusion | flops 6291456 | bytes 4728832 | tf_op jit(solution)/shard_map/rkd,rd->rk/dot_general | solution.py:109
  456.3 7.8 %all_to_all.26 = f32[4,256,8]{1,2,0:T(8,128)S(1)} all-to-all(f32[4,256,8]{1,2,0:T(8,128)S(1)} %broadcast_in_dim.98), channel_id=1, replica_groups=mesh['adapter'=32,'mp'=4] {'mp'}, dimensions={0} | all-to-all | bytes 65536 | tf_op jit(solution)/shard_map/all_to_all | solution.py:24
  464.2 0.1 copy.46
  464.3 5.8 %fusion.8 = f32[256,1,1024]{2,1,0:T(1,128)S(1)} fusion(f32[256,8,1]{1,2,0:T(1,128)S(1)} %copy.46, bf16[2048,1024]{1,0:T(8,128)(2,1)} %gather_fusion.1, pred[256,8]{1,0:T(8,128)(4,1)S(1)} %copy.38), kind=kOutput, calls=%fused_computation.17 | convolution fusion | flops 27262976 | bytes 5253120 | tf_op jit(solution)/shard_map/rk,rkd->rd/dot_general | solution.py:114
  470.1 1.1 fusion.19
  (33 shorter events, 0.9 us)
Async XLA Ops:
  6.5 417.6 %all-gather.2.cloned.1.call-start = ((), (), s32[]{:S(2)}) async-start(), calls=%async_computation.5 | async-start | bytes 17301504 | tf_op jit(solution)/shard_map/all_gather | solution.py:100
  13.2 31.6 %copy-start.1 = (bf16[1,1024,256]{2,1,0:T(8,128)(2,1)S(1)}, bf16[1,1024,256]{2,1,0:T(8,128)(2,1)}, u32[]{:S(2)}) copy-start(bf16[1,1024,256]{2,1,0:T(8,128)(2,1)} %param.8) | copy-start | bytes 1572868
  51.2 7.6 %copy-start.2 = (s32[256,8]{0,1:T(8,128)S(1)}, s32[256,8]{0,1:T(8,128)}, u32[]{:S(2)}) copy-start(s32[256,8]{0,1:T(8,128)} %param.7) | copy-start | bytes 24580
  51.3 232.1 %all-to-all-start = ((bf16[32,1,1024,256]{3,2,1,0:T(8,128)(2,1)}), bf16[32,1,1024,256]{3,2,1,0:T(8,128)(2,1)}, u32[]{:S(2)}, u32[]{:S(2)}) async-start(bf16[32,1,1024,256]{3,2,1,0:T(8,128)(2,1)} %stack.2), calls=%async_computation | async-start | bytes 33554432 | tf_op jit(solution)/shard_map/all_to_all | solution.py:12
  58.9 9.5 %copy-start = (bf16[256,1024]{1,0:T(8,128)(2,1)S(1)}, bf16[256,1024]{1,0:T(8,128)(2,1)}, u32[]{:S(2)}) copy-start(bf16[256,1024]{1,0:T(8,128)(2,1)} %param.6) | copy-start | bytes 1572868
  284.9 31.5 %all-to-all-start.3 = ((bf16[4,256,1024]{1,2,0:T(8,128)(2,1)}), bf16[4,256,1024]{1,2,0:T(8,128)(2,1)}, u32[]{:S(2)}, u32[]{:S(2)}) async-start(bf16[4,256,1024]{1,2,0:T(8,128)(2,1)} %broadcast_in_dim.97), calls=%async_computation.3 | async-start | bytes 4194304 | tf_op jit(solution)/shard_map/all_to_all | solution.py:24
  320.6 98.6 %all-to-all-start.1 = ((bf16[4,32,128,256]{3,2,1,0:T(8,128)(2,1)}), bf16[4,32,128,256]{3,2,1,0:T(8,128)(2,1)}, u32[]{:S(2)}, u32[]{:S(2)}) async-start(bf16[4,32,128,256]{3,2,1,0:T(8,128)(2,1)} %broadcast_in_dim.94), calls=%async_computation.1 | async-start | bytes 16777216 | tf_op jit(solution)/shard_map/all_to_all | solution.py:24
Sparse Core Ops, SparseCore 0:
  9.6 194.5 all-gather.1
